TPU v7x, 32 devices: a whole 2x2x4 slice. The times are simulated.
32 devices in a mesh: row: 8 (over y, x, core), col: 4 (over z).
Axes of the slice: x: 2, y: 2, z: 4, core: 2. Of those that a mesh axis runs over, the one named last changes fastest.
Arguments:
- alignment: float32 [192, 16, 64], P('row', 'col'), may hold values from -6 to 6
- pair_state: float32 [192, 192, 128], P('row', 'col'), may hold values from -6 to 6
- pair_weights: float32 [8, 192, 192], P(None, 'row', 'col'), may hold values from 0 to 1, as said below
- align_gain: float32 [64], replicated, may hold values from 0.5 to 2
- value_weight: float32 [64, 256], replicated, may hold values from -0.75 to 0.75
- gate_weight: float32 [64, 256], replicated, may hold values from -0.75 to 0.75
- output_weight: float32 [256, 64], replicated, may hold values from -0.375 to 0.375
- outer_gain: float32 [64], replicated, may hold values from 0.5 to 2
- left_weight: float32 [64, 32], replicated, may hold values from -0.75 to 0.75
- right_weight: float32 [64, 32], replicated, may hold values from -0.75 to 0.75
- outer_weight: float32 [1024, 128], replicated, may hold values from -0.75 to 0.75
- outer_bias: float32 [128], replicated, may hold values from -3 to 3
Outputs:
- alignment_out: float32 [192, 16, 64], P('row', 'col')
- pair_out: float32 [192, 192, 128], P('row', 'col')
Inputs may be any that keep to these rules, and one draw needn't show every extreme that they name: `pair_weights`: every entry is positive, and for each head and row token the weights over the 192 column tokens sum to one.
All inputs are finite; a program needn't handle non-finite values.
Results may differ from a plain program's by a relative error of at most 0.00011.
Values sent between devices are 32-bit elements; how exact they have to be, the bound alone decides.
A program may use at most 64 MiB of HBM per device.

v0:
```python
import jax
import jax.numpy as jnp
from jax import lax
from jax.sharding import PartitionSpec as P

PRECISE = lax.Precision.HIGHEST


def normalize(features, channel_gain):
    channel_mean = jnp.mean(features, axis=-1, keepdims=True)
    centered = features - channel_mean
    spread = jnp.mean(centered * centered, axis=-1, keepdims=True)
    return centered * lax.rsqrt(spread + 1e-05) * channel_gain


def on_device(
    alignment,
    pair_state,
    pair_weights,
    align_gain,
    value_weight,
    gate_weight,
    output_weight,
    outer_gain,
    left_weight,
    right_weight,
    outer_weight,
    outer_bias,
):
    head_count = pair_weights.shape[0]
    local_rows = alignment.shape[0]
    local_seqs = alignment.shape[1]
    channels = alignment.shape[2]
    normed = normalize(alignment, align_gain)
    flat_normed = normed.reshape(local_rows, local_seqs * channels)
    gathered = lax.all_gather(flat_normed, "row", axis=0, tiled=True)
    gathered = gathered.reshape(-1, local_seqs, channels)
    mixed_rows = jnp.einsum(
        "hij,jsc->ishc",
        lax.all_gather(pair_weights, "col", axis=2, tiled=True),
        gathered,
        precision=PRECISE,
    )
    per_head = value_weight.reshape(channels, head_count, -1)
    averaged = jnp.einsum("ishc,chd->ishd", mixed_rows, per_head, precision=PRECISE)
    gate_values = jax.nn.sigmoid(jnp.einsum("nsc,cd->nsd", normed, gate_weight, precision=PRECISE))
    gated_heads = gate_values * averaged.reshape(gate_values.shape)
    alignment_out = alignment + jnp.einsum(
        "nsd,dc->nsc", gated_heads, output_weight, precision=PRECISE
    )
    normed_out = normalize(alignment_out, outer_gain)
    left_side = jnp.einsum("nsc,cd->nsd", normed_out, left_weight, precision=PRECISE)
    right_side = jnp.einsum("nsc,cd->nsd", normed_out, right_weight, precision=PRECISE)
    factor_width = left_side.shape[2]
    columns = pair_state.shape[1]
    left_flat = left_side.transpose(1, 0, 2).reshape(local_seqs, local_rows * factor_width)
    right_rows = right_side.reshape(local_rows, local_seqs * factor_width)
    right_tokens = lax.all_gather(right_rows, "row", axis=0, tiled=True)
    right_tokens = right_tokens.reshape(-1, local_seqs, factor_width)
    right_columns = lax.all_to_all(right_tokens, "col", split_axis=0, concat_axis=1, tiled=True)
    right_all = right_columns.transpose(1, 0, 2)
    left_all = lax.all_gather(left_flat, "col", axis=0, tiled=True)
    sequences = left_all.shape[0]
    left_all = left_all.reshape(sequences, local_rows, factor_width)
    block_rows = 8
    left_blocks = left_all.reshape(
        sequences, local_rows // block_rows, block_rows, factor_width
    ).transpose(1, 2, 0, 3)

    def outer_block(left_block):
        product = jnp.einsum("isc,sjd->ijcd", left_block, right_all, precision=PRECISE) / sequences
        flattened = product.reshape(-1, factor_width * factor_width)
        projected = jnp.dot(
            flattened, outer_weight, precision=PRECISE, preferred_element_type=jnp.float32
        )
        return projected.reshape(block_rows, columns, -1)

    update = lax.map(outer_block, left_blocks).reshape(pair_state.shape)
    pair_out = pair_state + update + outer_bias
    return (alignment_out, pair_out)


def solution(mesh):
    return jax.shard_map(
        on_device,
        mesh=mesh,
        in_specs=(
            P("row", "col", None),
            P("row", "col", None),
            P(None, "row", "col"),
            P(),
            P(),
            P(),
            P(),
            P(),
            P(),
            P(),
            P(),
            P(),
        ),
        out_specs=(P("row", "col", None), P("row", "col", None)),
        check_vma=False,
    )
```

profile of v0, /device:TPU:0, one launch (start us, length us, event | category | flops | bytes accessed | tf_op | source)
XLA Modules:
  0.0 132.7 jit_solution(414286124162708641)
XLA Ops:
  0.6 0.0 copy-start
  0.7 1.0 reduce_sum.36
  1.7 1.0 multiply_reduce_fusion.1
  2.7 0.9 multiply_multiply_fusion.1
  3.6 0.1 reshape.65
  3.7 10.9 %all_gather.12 = f32[192,256]{1,0:T(8,128)S(1)} all-gather(f32[24,256]{1,0:T(8,128)S(1)} %reshape.65), channel_id=1, replica_groups=mesh['row'=8,'col'=4] {'row'}, dimensions={0}, use_global_device_ids=true | all-gather | bytes 221184 | tf_op jit(solution)/shard_map/all_gather | solution.py:36
  14.5 0.1 copy.88
  14.7 1.0 copy.89
  15.7 19.8 %all_gather.13 = f32[8,24,192]{1,0,2:T(8,128)S(1)} all-gather(f32[8,24,48]{1,0,2:T(8,128)S(1)} %copy.89), channel_id=1, replica_groups=mesh['row'=8,'col'=4] {'col'}, dimensions={2}, use_global_device_ids=true | all-gather | bytes 184320 | tf_op jit(solution)/shard_map/all_gather | solution.py:40
  35.5 0.9 copy.91
  36.5 1.5 %convolution_bitcast_fusion.2 = f32[24,4,8,64]{3,0,1,2:T(8,128)S(1)} fusion(f32[192,4,64,1]{0,2,1,3:T(8,128)S(1)} %bitcast.87, f32[8,24,192,1]{1,0,2,3:T(8,128)S(1)} %bitcast.83), kind=kOutput, calls=%fused_computation.8 | convolution fusion | flops 113246208 | bytes 540672 | tf_op jit(solution)/shard_map/hij,jsc->ishc/dot_general | solution.py:38
  38.0 0.5 convolution_bitcast_fusion.1
  38.5 0.2 copy.92
  38.7 0.2 reshape.68
  38.9 0.2 fusion.6
  39.2 0.3 fusion.21
  39.5 0.2 multiply_reduce_fusion
  39.7 0.2 fusion.12
  39.9 0.1 reshape.70
  40.0 9.2 %all_gather.15 = f32[192,128]{1,0:T(8,128)S(1)} all-gather(f32[24,128]{1,0:T(8,128)S(1)} %reshape.70), channel_id=1, replica_groups=mesh['row'=8,'col'=4] {'row'}, dimensions={0}, use_global_device_ids=true | all-gather | bytes 110592 | tf_op jit(solution)/shard_map/all_gather | solution.py:58
  49.3 0.1 copy.95
  49.4 0.2 copy.96
  49.6 0.9 reshape.87
  50.5 3.3 %all-to-all-start = ((f32[4,1,6144]{2,1,0:T(1,128)}), f32[4,1,6144]{2,1,0:T(1,128)S(1)}, u32[]{:S(2)}, u32[]{:S(2)}) async-start(f32[4,1,6144]{2,1,0:T(1,128)} %reshape.87), calls=%async_computation | async-start | bytes 196608 | tf_op jit(solution)/shard_map/all_to_all | solution.py:60
  53.8 0.6 copy.101
  54.4 0.2 convolution_bitcast_fusion.3
  54.7 0.1 reshape.73
  54.8 13.6 %all-gather = f32[4,4,768]{2,1,0:T(4,128)S(1)} all-gather(f32[1,4,768]{2,1,0:T(4,128)S(1)} %reshape.73), channel_id=1, replica_groups=mesh['row'=8,'col'=4] {'col'}, dimensions={0}, use_global_device_ids=true | all-gather | bytes 61440 | tf_op jit(solution)/shard_map/all_gather | solution.py:62
  68.4 0.1 reshape_reshape.3
  68.6 0.5 broadcast.66
  69.1 0.9 reduce
  70.0 0.2 reshape.88
  70.2 0.2 copy.98
  70.4 0.2 copy.100
  70.6 60.2 %while.10 = (s32[]{:T(128)}, f32[3,8,48,128]{3,2,1,0:T(8,128)}, f32[3,8,16,32]{3,1,0,2:T(8,128)S(1)}, f32[16,48,32]{1,0,2:T(8,128)S(1)}, f32[1024,128]{1,0:T(8,128)S(1)}, /*index=5*/s32[]{:T(128)}) while((s32[]{:T(128)}, f32[3,8,48,128]{3,2,1,0:T(8,128)}, f32[3,8,16,32]{3,1,0,2:T(8,128)S(1)}, f32[16,48,32]{1,0,2:T(8,128)S(1)}, ...), condition=%wide.region_5.6_spmd, body=%wide.region_4.5_spmd.sunk | while | flops 679870464 | bytes 10306121 | solution.py:78
  70.6 5.1 %multiply_bitcast_fusion.2 = f32[8,48,32,32]{1,2,3,0:T(8,128)} fusion(f32[16,48,32]{1,0,2:T(8,128)S(1)} %get-tuple-element.125, f32[1,8,16,32]{3,1,0,2:T(8,128)S(1)} %constant_dynamic-slice_fusion.2), kind=kOutput, calls=%fused_computation.clone.1 | convolution fusion | flops 75890688 | bytes 1687552 | tf_op jit(solution)/shard_map/while/body/eval_jaxpr/isc,sjd->ijcd/dot_general | solution.py:71
  75.7 7.9 %copy.122 = f32[8,48,32,32]{3,2,1,0:T(8,128)} copy(f32[8,48,32,32]{1,2,3,0:T(8,128)} %multiply_bitcast_fusion.2) | data formatting | bytes 3145728 | tf_op jit(solution)/shard_map/while/body/eval_jaxpr/div | solution.py:71
  83.5 5.0 %reshape.90 = f32[8,48,1024]{2,1,0:T(8,128)S(1)} reshape(f32[8,48,32,32]{3,2,1,0:T(8,128)} %copy.122) | data formatting | bytes 3145728 | tf_op jit(solution)/shard_map/reshape.27
  88.6 2.1 %fusion.34 = f32[3,8,48,128]{3,2,1,0:T(8,128)} fusion(f32[3,8,48,128]{3,2,1,0:T(8,128)} %get-tuple-element.117, s32[]{:T(128)} %get-tuple-element.116, f32[8,48,1024]{2,1,0:T(8,128)S(1)} %reshape.90, f32[1024,128]{1,0:T(8,128)S(1)} %get-tuple-element.126), kind=kOutput, calls=%fused_computation.2.clone.1 | convolution fusion | flops 603979776 | bytes 2294272 | tf_op jit(solution)/shard_map/while/body/eval_jaxpr/dot_general | solution.py:73
  90.7 5.1 %multiply_bitcast_fusion.2 = f32[8,48,32,32]{1,2,3,0:T(8,128)} fusion(f32[16,48,32]{1,0,2:T(8,128)S(1)} %get-tuple-element.125, f32[1,8,16,32]{3,1,0,2:T(8,128)S(1)} %constant_dynamic-slice_fusion.2), kind=kOutput, calls=%fused_computation.clone.1 | convolution fusion | flops 75890688 | bytes 1687552 | tf_op jit(solution)/shard_map/while/body/eval_jaxpr/isc,sjd->ijcd/dot_general | solution.py:71
  95.7 7.9 %copy.122 = f32[8,48,32,32]{3,2,1,0:T(8,128)} copy(f32[8,48,32,32]{1,2,3,0:T(8,128)} %multiply_bitcast_fusion.2) | data formatting | bytes 3145728 | tf_op jit(solution)/shard_map/while/body/eval_jaxpr/div | solution.py:71
  103.6 5.0 %reshape.90 = f32[8,48,1024]{2,1,0:T(8,128)S(1)} reshape(f32[8,48,32,32]{3,2,1,0:T(8,128)} %copy.122) | data formatting | bytes 3145728 | tf_op jit(solution)/shard_map/reshape.27
  108.6 2.1 %fusion.34 = f32[3,8,48,128]{3,2,1,0:T(8,128)} fusion(f32[3,8,48,128]{3,2,1,0:T(8,128)} %get-tuple-element.117, s32[]{:T(128)} %get-tuple-element.116, f32[8,48,1024]{2,1,0:T(8,128)S(1)} %reshape.90, f32[1024,128]{1,0:T(8,128)S(1)} %get-tuple-element.126), kind=kOutput, calls=%fused_computation.2.clone.1 | convolution fusion | flops 603979776 | bytes 2294272 | tf_op jit(solution)/shard_map/while/body/eval_jaxpr/dot_general | solution.py:73
  110.7 5.1 %multiply_bitcast_fusion.2 = f32[8,48,32,32]{1,2,3,0:T(8,128)} fusion(f32[16,48,32]{1,0,2:T(8,128)S(1)} %get-tuple-element.125, f32[1,8,16,32]{3,1,0,2:T(8,128)S(1)} %constant_dynamic-slice_fusion.2), kind=kOutput, calls=%fused_computation.clone.1 | convolution fusion | flops 75890688 | bytes 1687552 | tf_op jit(solution)/shard_map/while/body/eval_jaxpr/isc,sjd->ijcd/dot_general | solution.py:71
  115.8 7.9 %copy.122 = f32[8,48,32,32]{3,2,1,0:T(8,128)} copy(f32[8,48,32,32]{1,2,3,0:T(8,128)} %multiply_bitcast_fusion.2) | data formatting | bytes 3145728 | tf_op jit(solution)/shard_map/while/body/eval_jaxpr/div | solution.py:71
  123.6 5.0 %reshape.90 = f32[8,48,1024]{2,1,0:T(8,128)S(1)} reshape(f32[8,48,32,32]{3,2,1,0:T(8,128)} %copy.122) | data formatting | bytes 3145728 | tf_op jit(solution)/shard_map/reshape.27
  128.7 2.1 %fusion.34 = f32[3,8,48,128]{3,2,1,0:T(8,128)} fusion(f32[3,8,48,128]{3,2,1,0:T(8,128)} %get-tuple-element.117, s32[]{:T(128)} %get-tuple-element.116, f32[8,48,1024]{2,1,0:T(8,128)S(1)} %reshape.90, f32[1024,128]{1,0:T(8,128)S(1)} %get-tuple-element.126), kind=kOutput, calls=%fused_computation.2.clone.1 | convolution fusion | flops 603979776 | bytes 2294272 | tf_op jit(solution)/shard_map/while/body/eval_jaxpr/dot_general | solution.py:73
  130.8 1.9 %fusion.8 = f32[24,48,128]{2,1,0:T(8,128)} fusion(f32[24,48,128]{2,1,0:T(8,128)S(1)} %copy-done.3, f32[3,8,48,128]{3,2,1,0:T(8,128)} %get-tuple-element.29, f32[128]{0:T(128)S(1)} %copy-done.5), kind=kLoop, calls=%fused_computation.18 | loop fusion | flops 294912 | bytes 1769984 | tf_op jit(solution)/shard_map/add | solution.py:79
  (27 shorter events, 0.1 us)
Async XLA Ops:
  0.6 38.3 %copy-start = (f32[64,256]{1,0:T(8,128)S(1)}, f32[64,256]{1,0:T(8,128)}, u32[]{:S(2)}) copy-start(f32[64,256]{1,0:T(8,128)} %param.19) | copy-start | bytes 196612
  0.6 38.5 %copy-start.2 = (f32[24,4,64]{2,1,0:T(4,128)S(1)}, f32[24,4,64]{2,1,0:T(4,128)}, u32[]{:S(2)}) copy-start(f32[24,4,64]{2,1,0:T(4,128)} %param.14) | copy-start | bytes 73732
  0.7 38.5 %copy-start.4 = (f32[256,64]{0,1:T(8,128)S(1)}, f32[256,64]{0,1:T(8,128)}, u32[]{:S(2)}) copy-start(f32[256,64]{0,1:T(8,128)} %param.20) | copy-start | bytes 196612
  0.7 39.0 %copy-start.8 = (f32[64]{0:T(128)S(1)}, f32[64]{0:T(128)}, u32[]{:S(2)}) copy-start(f32[64]{0:T(128)} %param.21) | copy-start | bytes 772
  0.7 39.0 %copy-start.6 = (f32[64,32]{0,1:T(8,128)S(1)}, f32[64,32]{0,1:T(8,128)}, u32[]{:S(2)}) copy-start(f32[64,32]{0,1:T(8,128)} %param.23) | copy-start | bytes 24580
  3.7 50.8 %copy-start.7 = (f32[64,32]{0,1:T(8,128)S(1)}, f32[64,32]{0,1:T(8,128)}, u32[]{:S(2)}) copy-start(f32[64,32]{0,1:T(8,128)} %param.22) | copy-start | bytes 24580
  36.5 34.1 %copy-start.1 = (f32[1024,128]{1,0:T(8,128)S(1)}, f32[1024,128]{1,0:T(8,128)}, u32[]{:S(2)}) copy-start(f32[1024,128]{1,0:T(8,128)} %param.24) | copy-start | bytes 1572868
  50.5 18.1 %all-to-all-start = ((f32[4,1,6144]{2,1,0:T(1,128)}), f32[4,1,6144]{2,1,0:T(1,128)S(1)}, u32[]{:S(2)}, u32[]{:S(2)}) async-start(f32[4,1,6144]{2,1,0:T(1,128)} %reshape.87), calls=%async_computation | async-start | bytes 196608 | tf_op jit(solution)/shard_map/all_to_all | solution.py:60
  70.5 60.2 %copy-start.3 = (f32[24,48,128]{2,1,0:T(8,128)S(1)}, f32[24,48,128]{2,1,0:T(8,128)}, u32[]{:S(2)}) copy-start(f32[24,48,128]{2,1,0:T(8,128)} %param.15) | copy-start | bytes 1769476
  70.5 60.2 %copy-start.5 = (f32[128]{0:T(128)S(1)}, f32[128]{0:T(128)}, u32[]{:S(2)}) copy-start(f32[128]{0:T(128)} %param.25) | copy-start | bytes 1540
where the time goes:
time: 134 us; the launch traced here: 133 us
  blocking collectives  53.6 us (40%)
  local copies, waits for them, and re-layouts  44.6 us (33%)
  matrix products  24.4 us (18%)
  other arithmetic  5.88 us (4%)
  starting transfers between devices  3.3 us (2%)
    div x3, local copies, waits for them, and re-layouts, outer_block(): jnp.einsum('isc,sjd->ijcd', left_block, right_all, precision=PRECISE)  23.6 us
    all_gather x1, blocking collectives, on_device(): lax.all_gather(pair_weights, 'col', axis=2, tiled=True)  19.8 us
    dot_general x3, matrix products, outer_block(): jnp.einsum('isc,sjd->ijcd', left_block, right_all, precision=PRECISE)  15.2 us
    another operation x3, local copies, waits for them, and re-layouts  15.1 us
    all_gather x1, blocking collectives, on_device(): left_all = lax.all_gather(left_flat, 'col', axis=0, tiled=True)  13.6 us
    all_gather x1, blocking collectives, on_device(): gathered = lax.all_gather(flat_normed, 'row', axis=0, tiled=True)  10.9 us
    all_gather x1, blocking collectives, on_device(): right_tokens = lax.all_gather(right_rows, 'row', axis=0, tiled=True)  9.21 us
    dot_general x3, matrix products, outer_block(): jnp.dot(flattened, outer_weight, precision=PRECISE, preferred_element_typ...  6.23 us
  transfers between devices with their start and end apart: 1, of which 0 were waited for; matrix products, arithmetic and copies ran while one was open for 1% of the time, Pallas kernels for 0%

commit v1 on v0

v1 whole, which is shorter than its diff:
```python
import functools

import jax
import jax.numpy as jnp
from jax import lax
from jax.experimental import pallas as pl
from jax.experimental.pallas import tpu as pltpu
from jax.sharding import PartitionSpec as P

MESH = pl.DeviceIdType.MESH
F32, BF16 = jnp.float32, jnp.bfloat16


def dot(a, b):
    return jnp.dot(a, b, preferred_element_type=F32)


def split(a):
    hi = a.astype(BF16)
    return hi, (a - hi.astype(F32)).astype(BF16)


def stack(a):
    hi = a.astype(BF16).astype(F32)
    return jnp.concatenate([hi, a - hi], axis=0).astype(BF16)


def fold_rows(a):
    half = a.shape[0] // 2
    return a[:half] + a[half:]


def dot3(a, bh, bl):
    return fold_rows(dot(stack(a), bh)) + dot(a.astype(BF16), bl)


def iotas(shape):
    return (
        lax.broadcasted_iota(jnp.int32, shape, 0),
        lax.broadcasted_iota(jnp.int32, shape, 1),
    )


def div(x, n):
    return x >> (n.bit_length() - 1) if n & (n - 1) == 0 else lax.div(x, jnp.int32(n))


def rem(x, n):
    return x & (n - 1) if n & (n - 1) == 0 else lax.rem(x, jnp.int32(n))


def block_diagonal(w, copies):
    rows, cols = w.shape
    wide = jnp.concatenate([w] * copies, axis=1)
    tall = jnp.concatenate([wide] * copies, axis=0)
    r, c = iotas(tall.shape)
    return jnp.where(div(r, rows) == div(c, cols), tall, 0.0)


def kernel(
    n_row, n_col, heads, fold, columns,
    x_ref, w_ref, ag_ref, v_ref, g_ref, o_ref, og_ref, lw_ref, rw_ref, ow_hbm,
    a_out, upd_out,
    xbuf, wbuf, lr, lbuf, rbuf, ow, wp, perm, lp, th, tl,
    bd_v, bd_g, bd_o, bd_lr,
    sx, rx, sw, rws, sl, rl, sr, rr, ow_sem,
):
    r, c = lax.axis_index("row"), lax.axis_index("col")
    rows, width = x_ref.shape
    channels = v_ref.shape[0]
    seqs = width // channels
    factor = lw_ref.shape[1]
    lanes = seqs * factor
    all_seqs = seqs * n_col
    per = columns // rows
    home = r // per
    slot = r % per
    is_home = home == c
    mine = (r, c)

    load_ow = pltpu.make_async_copy(ow_hbm, ow, ow_sem)
    load_ow.start()

    barrier = pltpu.get_barrier_semaphore()
    for k in range(1, n_row):
        pl.semaphore_signal(barrier, 1, device_id=((r + k) % n_row, c), device_id_type=MESH)
    for k in range(1, n_col):
        pl.semaphore_signal(barrier, 1, device_id=(r, (c + k) % n_col), device_id_type=MESH)
    for a in range(per):
        for k in range(n_col):
            src_r = c * per + a

            @pl.when(jnp.logical_and(src_r != r, k != c))
            def _():
                pl.semaphore_signal(barrier, 1, device_id=(src_r, jnp.int32(k)), device_id_type=MESH)

    @pl.when(is_home)
    def _():
        pl.semaphore_wait(barrier, n_row - 1 + n_col - 1)

    @pl.when(jnp.logical_not(is_home))
    def _():
        pl.semaphore_wait(barrier, n_row - 1 + n_col - 1 + n_row - 1)

    def remote(src, dst, send, recv, device):
        return pltpu.make_async_remote_copy(
            src_ref=src, dst_ref=dst, send_sem=send, recv_sem=recv,
            device_id=device, device_id_type=MESH,
        )

    sends = []
    for k in range(1, n_col):
        cp = remote(w_ref, wbuf.at[c], sw.at[k], rws.at[c], (r, (c + k) % n_col))
        cp.start()
        sends.append(cp)
    for k in range(1, n_row):
        cp = remote(x_ref, xbuf.at[r], sx.at[k], rx.at[r], ((r + k) % n_row, c))
        cp.start()
        sends.append(cp)

    xbuf[r] = x_ref[...]
    wbuf[c] = w_ref[...]
    part = v_ref.shape[1] // fold
    for a in range(fold):
        lo_l, hi_l = a * part, (a + 1) * part
        for ref, bd, w in (
            (v_ref, bd_v, v_ref[:, lo_l:hi_l]),
            (g_ref, bd_g, g_ref[:, lo_l:hi_l]),
            (o_ref, bd_o, o_ref[lo_l:hi_l, :]),
        ):
            h, l = split(block_diagonal(w, seqs))
            bd[a, 0] = h
            bd[a, 1] = l
    h, l = split(
        jnp.concatenate(
            [block_diagonal(lw_ref[...], seqs), block_diagonal(rw_ref[...], seqs)], axis=1
        )
    )
    bd_lr[0] = h
    bd_lr[1] = l
    pr, pc = iotas(perm.shape)
    perm[...] = jnp.where(
        pr == rem(pc, all_seqs) * factor + div(pc, all_seqs), 1.0, 0.0
    ).astype(BF16)

    mr, mc = iotas((width, width))
    mean_of = jnp.where(div(mr, channels) == div(mc, channels), 1.0 / channels, 0.0).astype(BF16)

    def normalize(x, gain):
        cen = x - fold_rows(dot(stack(x), mean_of))
        var = fold_rows(dot(stack(cen * cen), mean_of))
        return cen * lax.rsqrt(var + 1e-05) * gain

    gain = jnp.concatenate([ag_ref[...]] * seqs, axis=1)
    out_gain = jnp.concatenate([og_ref[...]] * seqs, axis=1)
    own = normalize(x_ref[...], gain)
    gates = [
        1.0 / (1.0 + jnp.exp(-dot3(own, bd_g[a, 0], bd_g[a, 1]))) for a in range(fold)
    ]

    load_ow.wait()
    z = ow.shape[1]
    for d in range(factor):
        h, l = split(ow[pl.ds(d, factor, stride=factor), :])
        wp[:, d * z : (d + 1) * z] = jnp.concatenate([h, h, l], axis=0)

    for k in range(1, n_row):
        s = (r + k) % n_row
        remote(x_ref, xbuf.at[s], sx.at[k], rx.at[s], (s, c)).wait_recv()
    nh, nl = split(normalize(xbuf[...].reshape(n_row * rows, width), gain))
    kpad = w_ref.shape[1] - fold * columns

    def spread(n):
        parts = []
        for cc in range(n_col):
            blk = n[cc * columns : (cc + 1) * columns]
            for a in range(fold):
                parts.append(
                    jnp.concatenate(
                        [blk if b == a else jnp.zeros_like(blk) for b in range(fold)], axis=1
                    )
                )
            if kpad:
                parts.append(jnp.zeros((kpad, fold * width), BF16))
        return jnp.concatenate(parts, axis=0)

    sh, sl_ = spread(nh), spread(nl)
    for k in range(1, n_col):
        s = (c + k) % n_col
        remote(w_ref, wbuf.at[s], sw.at[k], rws.at[s], (r, s)).wait_recv()
    wide = jnp.concatenate([wbuf[cc] for cc in range(n_col)], axis=1)
    mixed = dot3(wide, sh, sl_)
    hpart = heads // fold
    head_dim = part // hpart
    res = x_ref[...]
    for a in range(fold):
        full = dot3(mixed[:, a * width : (a + 1) * width], bd_v[a, 0], bd_v[a, 1])
        _, lane = iotas((rows, seqs * part))
        head_of = rem(div(lane, head_dim), hpart)
        avg = jnp.zeros((rows, seqs * part), F32)
        for hh in range(hpart):
            avg = jnp.where(head_of == hh, full[hh * rows : (hh + 1) * rows], avg)
        res = res + dot3(gates[a] * avg, bd_o[a, 0], bd_o[a, 1])
    a_out[...] = res
    both = dot3(normalize(res, out_gain), bd_lr[0], bd_lr[1])
    lr[0] = both[:, :lanes]
    lr[1] = both[:, lanes:]

    for k in range(1, n_col):
        cp = remote(lr.at[0], lbuf.at[c], sl.at[k], rl.at[c], (r, (c + k) % n_col))
        cp.start()
        sends.append(cp)
    for k in range(1, n_row):
        cp = remote(lr.at[1], rbuf.at[slot, c], sr.at[k], rr.at[slot, c], ((r + k) % n_row, home))
        cp.start()
        sends.append(cp)
    to_home = remote(lr.at[1], rbuf.at[slot, c], sr.at[0], rr.at[slot, c], (r, home))

    @pl.when(jnp.logical_not(is_home))
    def _():
        to_home.start()

    @pl.when(is_home)
    def _():
        rbuf[slot, c] = both[:, lanes:]

    lbuf[c] = both[:, :lanes]
    for k in range(1, n_col):
        s = (c + k) % n_col
        remote(lr.at[0], lbuf.at[s], sl.at[k], rl.at[s], (r, s)).wait_recv()
    for cc in range(n_col):
        blk = lbuf[cc]
        hi = blk.astype(BF16).astype(F32)
        lo = blk - hi
        for s in range(seqs):
            cut = slice(s * factor, (s + 1) * factor)
            pieces = [hi[:, cut], lo[:, cut], hi[:, cut], jnp.zeros((rows, lp.shape[1] - 3 * factor), F32)]
            lp[pl.ds(cc * seqs + s, rows, stride=all_seqs), :] = jnp.concatenate(pieces, axis=1)

    pairs = th.shape[0]
    block = pairs * 2

    def make_t(first):
        left = lp[pl.ds(pl.multiple_of(first * all_seqs, 8), block * all_seqs), :][
            :, : 3 * factor
        ].astype(BF16)
        for d in range(0, factor, 2):
            t = dot(left, wp[:, d * z : (d + 2) * z])
            for e in range(2):
                h, l = split(t[:, e * z : (e + 1) * z])
                h = h.reshape(pairs, 2, all_seqs, z)
                l = l.reshape(pairs, 2, all_seqs, z)
                at = slice((d + e) * all_seqs, (d + e + 1) * all_seqs)
                for q in range(2):
                    th[:, at, q * z : (q + 1) * z] = h[:, q]
                    tl[:, at, q * z : (q + 1) * z] = l[:, q]

    make_t(0)

    for a in range(per):
        for cc in range(n_col):

            @pl.when(jnp.logical_not(jnp.logical_and(c * per + a == r, cc == c)))
            def _():
                remote(
                    lr.at[1], rbuf.at[a, cc], sr.at[0], rr.at[a, cc], (c * per + a, jnp.int32(cc))
                ).wait_recv()

    right = jnp.concatenate(
        [jnp.concatenate([rbuf[a, cc] for cc in range(n_col)], axis=1) for a in range(per)], axis=0
    ) * (1.0 / all_seqs)
    right2 = dot(stack(right), perm[...]).astype(BF16)
    right1 = right2[:columns]

    def finish(first):
        for q in range(pairs):
            u = fold_rows(dot(right2, th[q])) + dot(right1, tl[q])
            upd_out[first + 2 * q] = u[:, :z]
            upd_out[first + 2 * q + 1] = u[:, z:]

    finish(0)
    if rows > block:

        def step(i, _):
            make_t(i * block)
            finish(i * block)
            return 0

        lax.fori_loop(1, rows // block, step, 0)

    for cp in sends:
        cp.wait_send()

    @pl.when(jnp.logical_not(is_home))
    def _():
        to_home.wait_send()


def on_device(
    n_row, n_col,
    alignment, pair_state, pair_weights, align_gain, value_weight, gate_weight,
    output_weight, outer_gain, left_weight, right_weight, outer_weight, outer_bias,
):
    heads = pair_weights.shape[0]
    rows, seqs, channels = alignment.shape
    columns = pair_state.shape[1]
    z = pair_state.shape[2]
    factor = left_weight.shape[1]
    hidden = value_weight.shape[1]
    all_seqs = seqs * n_col
    width = seqs * channels
    fold = max(1, 128 // columns)
    while heads % fold:
        fold -= 1
    wide = -(-fold * columns // 128) * 128
    x2 = alignment.reshape(rows, width)
    w2 = pair_weights.reshape(fold, heads // fold * rows, columns)
    w2 = jnp.concatenate([w2[a] for a in range(fold)], axis=1)
    w2 = jnp.pad(w2, ((0, 0), (0, wide - fold * columns)))
    block = 2
    for b in range(2, rows + 1, 2):
        if rows % b == 0 and b * all_seqs <= 384:
            block = b
    per = columns // rows
    part = hidden // fold
    vmem = pl.BlockSpec(memory_space=pltpu.VMEM)
    dma = pltpu.SemaphoreType.DMA
    a_out, update = pl.pallas_call(
        functools.partial(kernel, n_row, n_col, heads, fold, columns),
        name="msa_block",
        out_shape=(
            jax.ShapeDtypeStruct((rows, width), F32),
            jax.ShapeDtypeStruct((rows, columns, z), F32),
        ),
        in_specs=[vmem] * 9 + [pl.BlockSpec(memory_space=pl.ANY)],
        out_specs=(vmem, vmem),
        scratch_shapes=[
            pltpu.VMEM((n_row, rows, width), F32),
            pltpu.VMEM((n_col, w2.shape[0], wide), F32),
            pltpu.VMEM((2, rows, seqs * factor), F32),
            pltpu.VMEM((n_col, rows, seqs * factor), F32),
            pltpu.VMEM((per, n_col, rows, seqs * factor), F32),
            pltpu.VMEM(outer_weight.shape, F32),
            pltpu.VMEM((3 * factor, factor * z), BF16),
            pltpu.VMEM((all_seqs * factor, all_seqs * factor), BF16),
            pltpu.VMEM((rows * all_seqs, 128), F32),
            pltpu.VMEM((block // 2, all_seqs * factor, 2 * z), BF16),
            pltpu.VMEM((block // 2, all_seqs * factor, 2 * z), BF16),
            pltpu.VMEM((fold, 2, width, seqs * part), BF16),
            pltpu.VMEM((fold, 2, width, seqs * part), BF16),
            pltpu.VMEM((fold, 2, seqs * part, width), BF16),
            pltpu.VMEM((2, width, 2 * seqs * factor), BF16),
            dma((n_row,)),
            dma((n_row,)),
            dma((n_col,)),
            dma((n_col,)),
            dma((n_col,)),
            dma((n_col,)),
            dma((n_row,)),
            dma((per, n_col)),
            dma(()),
        ],
        compiler_params=pltpu.CompilerParams(collective_id=0, has_side_effects=True),
    )(
        x2, w2, align_gain.reshape(1, -1), value_weight, gate_weight, output_weight,
        outer_gain.reshape(1, -1), left_weight, right_weight, outer_weight,
    )
    pair_out = pair_state + update + outer_bias
    return (a_out.reshape(alignment.shape), pair_out)


def solution(mesh):
    n_row, n_col = mesh.shape["row"], mesh.shape["col"]
    return jax.shard_map(
        functools.partial(on_device, n_row, n_col),
        mesh=mesh,
        in_specs=(
            P("row", "col", None),
            P("row", "col", None),
            P(None, "row", "col"),
        )
        + (P(),) * 9,
        out_specs=(P("row", "col", None), P("row", "col", None)),
        check_vma=False,
    )
```

time: 134 us -> 33.4 us (0.25)
  blocking collectives: 53.6 us -> 0 us
  local copies, waits for them, and re-layouts: 44.6 us -> 5.17 us
  Pallas kernels: 0 us -> 24.6 us
  matrix products: 24.4 us -> 0 us
  starting transfers between devices: 3.3 us -> 0 us
  other arithmetic: 5.88 us -> 2.65 us
    all_gather x4 -> x0, blocking collectives: 53.6 us -> none  [the longest x1 19.8 us: on_device(): lax.all_gather(pair_weights, 'col', axis=2, tiled=True)]
    pallas_call x0 -> x1, Pallas kernels: none -> 24.6 us  [on_device(): pl.pallas_call(functools.partial(kernel, n_row, n_col, heads, fold, colum...]
    dot_general x12 -> x0, matrix products: 24.4 us -> none  [the longest x3 15.2 us: outer_block(): jnp.einsum('isc,sjd->ijcd', left_block, right_all, precision=PRECISE)]
    div x3 -> x0, local copies, waits for them, and re-layouts: 23.6 us -> none  [outer_block(): jnp.einsum('isc,sjd->ijcd', left_block, right_all, precision=PRECISE)]
    another operation x4 -> x0, local copies, waits for them, and re-layouts: 15.2 us -> none
    all_to_all x1 -> x0, starting transfers between devices: 3.3 us -> none  [on_device(): lax.all_to_all(right_tokens, 'col', split_axis=0, concat_axis=1, tiled=True)]
    reduce_sum x3 -> x0, other arithmetic: 2.1 us -> none  [the longest x2 1.14 us: normalize(): spread = jnp.mean(centered * centered, axis=-1, keepdims=True)]
    unnamed x24 -> x17, local copies, waits for them, and re-layouts: 3.85 us -> 2.93 us
  transfers between devices with their start and end apart: 1 -> 0, of which waited for: 0 -> 0; matrix products, arithmetic and copies ran while one was open for 1% -> 0% of each run, Pallas kernels for 0% -> 0%
where the time goes in v1:
time: 33.4 us; the launch traced here: 33.1 us
  Pallas kernels  24.6 us (74%)
  local copies, waits for them, and re-layouts  5.17 us (15%)
  other arithmetic  2.65 us (8%)
  between operations  0.67 us (2%)
    pallas_call x1, Pallas kernels, on_device(): pl.pallas_call(functools.partial(kernel, n_row, n_col, heads, fold, colum...  24.6 us
    unnamed x17, local copies, waits for them, and re-layouts  2.93 us
    add x1, other arithmetic, on_device(): pair_out = pair_state + update + outer_bias  1.95 us
    slice x1, local copies, waits for them, and re-layouts, on_device(): w2 = jnp.concatenate([w2[a] for a in range(fold)], axis=1)  0.83 us
    concatenate x1, other arithmetic, on_device(): w2 = jnp.concatenate([w2[a] for a in range(fold)], axis=1)  0.71 us
    reshape x1, local copies, waits for them, and re-layouts, on_device(): return (a_out.reshape(alignment.shape), pair_out)  0.7 us
    reshape x1, local copies, waits for them, and re-layouts, on_device(): x2 = alignment.reshape(rows, width)  0.7 us

profile of v1, /device:TPU:0, one launch (start us, length us, event | category | flops | bytes accessed | tf_op | source)
XLA Modules:
  0.0 33.1 jit_solution(14211648568731510856)
XLA Ops:
  0.6 0.8 %fusion = (f32[4,24,48]{2,1,0:T(8,128)S(1)}, f32[4,24,48]{2,1,0:T(8,128)S(1)}) fusion(f32[8,24,48]{2,1,0:T(8,128)} %param.14), kind=kLoop, calls=%fused_computation.3 | loop fusion | bytes 73728 | tf_op jit(solution)/shard_map/slice | solution.py:318
  1.5 0.0 copy-start.1
  1.5 0.7 %select_maximum_fusion.w_ref = f32[96,128]{1,0:T(8,128)} fusion(f32[96,48]{1,0:T(8,128)S(1)} %bitcast.5, f32[96,48]{1,0:T(8,128)S(1)} %bitcast.4), kind=kLoop, calls=%fused_computation.1 | loop fusion | flops 49152 | bytes 86016 | tf_op jit(solution)/shard_map/concatenate | solution.py:318
  2.2 0.1 copy-done.1
  2.3 0.0 copy-start.4
  2.3 0.0 copy-start.5
  2.3 0.0 copy-start.2
  2.3 0.8 %copy.14.o_ref = f32[256,64]{1,0:T(8,128)} copy(f32[256,64]{0,1:T(8,128)S(1)} %copy-done.1) | data formatting | bytes 131072 | tf_op args[6]
  3.1 0.0 copy-done.4
  3.1 0.0 copy-start
  3.1 0.7 %copy.15.lw_ref = f32[64,32]{1,0:T(8,128)} copy(f32[64,32]{0,1:T(8,128)S(1)} %copy-done.4) | data formatting | bytes 16384 | tf_op args[8]
  3.8 0.0 copy-done.5
  3.8 0.7 %copy.16.rw_ref = f32[64,32]{1,0:T(8,128)} copy(f32[64,32]{0,1:T(8,128)S(1)} %copy-done.5) | data formatting | bytes 16384 | tf_op args[9]
  4.5 0.0 copy-done.2
  4.5 0.7 %reshape.22.x_ref = f32[24,256]{1,0:T(8,128)} reshape(f32[24,4,64]{2,1,0:T(4,128)S(1)} %copy-done.2) | data formatting | bytes 49152 | tf_op jit(solution)/shard_map/reshape | solution.py:316
  5.2 24.6 %msa_block.1 = (f32[24,256]{1,0:T(8,128)}, f32[24,48,128]{2,1,0:T(8,128)}) custom-call(f32[24,256]{1,0:T(8,128)} %reshape.22.x_ref, f32[96,128]{1,0:T(8,128)} %select_maximum_fusion.w_ref, f32[1,64]{1,0:T(1,128)} %bitcast.6, f32[64,256]{1,0:T(8,128)} %v_ref.1, f32[64,256]{1,0:T(8,128)} %g_ref.1, f32[256,64]{1,0:T(8,128)} %copy.14.o_ref, f32[1,64]{1,0:T(1,128)} %bitcast.7, ...), custom_call_target="tpu_custom_call" | custom-call | tf_op jit(solution)/shard_map/msa_block/pallas_call | solution.py:328
  29.8 0.0 copy-start.6
  29.8 0.0 copy-done
  29.8 0.6 %copy-done.6 = f32[128]{0:T(128)S(1)} copy-done((f32[128]{0:T(128)S(1)}, f32[128]{0:T(128)}, u32[]{:S(2)}) %copy-start.6) | copy-done | bytes 536
  30.4 0.0 copy-start.3
  30.4 1.9 %add_add_fusion = f32[24,48,128]{2,1,0:T(8,128)} fusion(f32[24,48,128]{2,1,0:T(8,128)S(1)} %copy-done, f32[24,48,128]{2,1,0:T(8,128)} %get-tuple-element.5, f32[128]{0:T(128)S(1)} %copy-done.6), kind=kLoop, calls=%fused_computation | loop fusion | flops 294912 | bytes 1769984 | tf_op jit(solution)/shard_map/add | solution.py:368
  32.4 0.0 copy-done.3
  32.4 0.7 %reshape.25 = f32[24,4,64]{2,1,0:T(4,128)} reshape(f32[24,256]{1,0:T(8,128)S(1)} %copy-done.3) | data formatting | bytes 49152 | tf_op jit(solution)/shard_map/reshape | solution.py:369
Async XLA Ops:
  1.5 0.8 %copy-start.1 = (f32[256,64]{0,1:T(8,128)S(1)}, f32[256,64]{0,1:T(8,128)}, u32[]{:S(2)}) copy-start(f32[256,64]{0,1:T(8,128)} %param.18) | copy-start | bytes 196612
  2.3 0.8 %copy-start.4 = (f32[64,32]{0,1:T(8,128)S(1)}, f32[64,32]{0,1:T(8,128)}, u32[]{:S(2)}) copy-start(f32[64,32]{0,1:T(8,128)} %param.20) | copy-start | bytes 24580
  2.3 1.5 %copy-start.5 = (f32[64,32]{0,1:T(8,128)S(1)}, f32[64,32]{0,1:T(8,128)}, u32[]{:S(2)}) copy-start(f32[64,32]{0,1:T(8,128)} %param.21) | copy-start | bytes 24580
  2.3 2.2 %copy-start.2 = (f32[24,4,64]{2,1,0:T(4,128)S(1)}, f32[24,4,64]{2,1,0:T(4,128)}, u32[]{:S(2)}) copy-start(f32[24,4,64]{2,1,0:T(4,128)} %param.12) | copy-start | bytes 73732
  3.1 26.7 %copy-start = (f32[24,48,128]{2,1,0:T(8,128)S(1)}, f32[24,48,128]{2,1,0:T(8,128)}, u32[]{:S(2)}) copy-start(f32[24,48,128]{2,1,0:T(8,128)} %param.13) | copy-start | bytes 1769476
  29.8 0.7 %copy-start.6 = (f32[128]{0:T(128)S(1)}, f32[128]{0:T(128)}, u32[]{:S(2)}) copy-start(f32[128]{0:T(128)} %param.23) | copy-start | bytes 1540
  30.4 2.0 %copy-start.3 = (f32[24,256]{1,0:T(8,128)S(1)}, f32[24,256]{1,0:T(8,128)}, u32[]{:S(2)}) copy-start(f32[24,256]{1,0:T(8,128)} %get-tuple-element.4) | copy-start | bytes 73732

commit v2 on v1

--- a/solution.py
+++ b/solution.py
@@ -57,19 +57,19 @@
     return jnp.where(div(r, rows) == div(c, cols), tall, 0.0)
 
 
-def kernel(
-    n_row, n_col, heads, fold, columns,
-    x_ref, w_ref, ag_ref, v_ref, g_ref, o_ref, og_ref, lw_ref, rw_ref, ow_hbm,
-    a_out, upd_out,
-    xbuf, wbuf, lr, lbuf, rbuf, ow, wp, perm, lp, th, tl,
+def kernel(n_row, n_col, heads, fold, columns, *refs):
+    inputs, (a_out, upd_out), local = refs[:11], refs[11:13], refs[13:24]
+    x_in, w_in, ag_ref, v_ref, g_ref, ot_ref, og_ref, lwt_ref, rwt_ref, bias_ref, ow = local
+    (
+    x_ref, w_ref, xbuf, wbuf, lr, lbuf, rbuf, wp, perm, lp, th, tl,
     bd_v, bd_g, bd_o, bd_lr,
-    sx, rx, sw, rws, sl, rl, sr, rr, ow_sem,
-):
+    sx, rx, sw, rws, sl, rl, sr, rr, in_sem,
+    ) = refs[24:]
     r, c = lax.axis_index("row"), lax.axis_index("col")
     rows, width = x_ref.shape
     channels = v_ref.shape[0]
     seqs = width // channels
-    factor = lw_ref.shape[1]
+    factor = lwt_ref.shape[0]
     lanes = seqs * factor
     all_seqs = seqs * n_col
     per = columns // rows
@@ -78,8 +78,9 @@
     is_home = home == c
     mine = (r, c)
 
-    load_ow = pltpu.make_async_copy(ow_hbm, ow, ow_sem)
-    load_ow.start()
+    loads = [pltpu.make_async_copy(a, b, in_sem.at[k]) for k, (a, b) in enumerate(zip(inputs, local))]
+    for load in loads:
+        load.start()
 
     barrier = pltpu.get_barrier_semaphore()
     for k in range(1, n_row):
@@ -93,6 +94,16 @@
             @pl.when(jnp.logical_and(src_r != r, k != c))
             def _():
                 pl.semaphore_signal(barrier, 1, device_id=(src_r, jnp.int32(k)), device_id_type=MESH)
+
+    loads[0].wait()
+    loads[1].wait()
+    x_ref[...] = jnp.concatenate([x_in[:, s, :] for s in range(seqs)], axis=1)
+    half = w_ref.shape[0]
+    packed = [w_in[a * half : (a + 1) * half, :] for a in range(fold)]
+    kpad = w_ref.shape[1] - fold * columns
+    if kpad:
+        packed.append(jnp.zeros((half, kpad), F32))
+    w_ref[...] = jnp.concatenate(packed, axis=1)
 
     @pl.when(is_home)
     def _():
@@ -120,20 +131,23 @@
 
     xbuf[r] = x_ref[...]
     wbuf[c] = w_ref[...]
+    for load in loads[2:]:
+        load.wait()
     part = v_ref.shape[1] // fold
+    o_w = ot_ref[...].T
     for a in range(fold):
         lo_l, hi_l = a * part, (a + 1) * part
         for ref, bd, w in (
             (v_ref, bd_v, v_ref[:, lo_l:hi_l]),
             (g_ref, bd_g, g_ref[:, lo_l:hi_l]),
-            (o_ref, bd_o, o_ref[lo_l:hi_l, :]),
+            (ot_ref, bd_o, o_w[lo_l:hi_l, :]),
         ):
             h, l = split(block_diagonal(w, seqs))
             bd[a, 0] = h
             bd[a, 1] = l
     h, l = split(
         jnp.concatenate(
-            [block_diagonal(lw_ref[...], seqs), block_diagonal(rw_ref[...], seqs)], axis=1
+            [block_diagonal(ref[...].T, seqs) for ref in (lwt_ref, rwt_ref)], axis=1
         )
     )
     bd_lr[0] = h
@@ -158,7 +172,6 @@
         1.0 / (1.0 + jnp.exp(-dot3(own, bd_g[a, 0], bd_g[a, 1]))) for a in range(fold)
     ]
 
-    load_ow.wait()
     z = ow.shape[1]
     for d in range(factor):
         h, l = split(ow[pl.ds(d, factor, stride=factor), :])
@@ -168,7 +181,6 @@
         s = (r + k) % n_row
         remote(x_ref, xbuf.at[s], sx.at[k], rx.at[s], (s, c)).wait_recv()
     nh, nl = split(normalize(xbuf[...].reshape(n_row * rows, width), gain))
-    kpad = w_ref.shape[1] - fold * columns
 
     def spread(n):
         parts = []
@@ -272,9 +284,11 @@
     right2 = dot(stack(right), perm[...]).astype(BF16)
     right1 = right2[:columns]
 
+    bias2 = jnp.concatenate([bias_ref[...]] * 2, axis=1)
+
     def finish(first):
         for q in range(pairs):
-            u = fold_rows(dot(right2, th[q])) + dot(right1, tl[q])
+            u = fold_rows(dot(right2, th[q])) + dot(right1, tl[q]) + bias2
             upd_out[first + 2 * q] = u[:, :z]
             upd_out[first + 2 * q + 1] = u[:, z:]
 
@@ -313,10 +327,7 @@
     while heads % fold:
         fold -= 1
     wide = -(-fold * columns // 128) * 128
-    x2 = alignment.reshape(rows, width)
-    w2 = pair_weights.reshape(fold, heads // fold * rows, columns)
-    w2 = jnp.concatenate([w2[a] for a in range(fold)], axis=1)
-    w2 = jnp.pad(w2, ((0, 0), (0, wide - fold * columns)))
+    half = heads // fold * rows
     block = 2
     for b in range(2, rows + 1, 2):
         if rows % b == 0 and b * all_seqs <= 384:
@@ -325,22 +336,29 @@
     part = hidden // fold
     vmem = pl.BlockSpec(memory_space=pltpu.VMEM)
     dma = pltpu.SemaphoreType.DMA
+    operands = (
+        alignment, pair_weights.reshape(heads * rows, columns), align_gain.reshape(1, -1),
+        value_weight, gate_weight, output_weight.T, outer_gain.reshape(1, -1),
+        left_weight.T, right_weight.T, outer_bias.reshape(1, -1), outer_weight,
+    )
     a_out, update = pl.pallas_call(
         functools.partial(kernel, n_row, n_col, heads, fold, columns),
         name="msa_block",
         out_shape=(
             jax.ShapeDtypeStruct((rows, width), F32),
-            jax.ShapeDtypeStruct((rows, columns, z), F32),
+            pltpu.VMEM((rows, columns, z), F32),
         ),
-        in_specs=[vmem] * 9 + [pl.BlockSpec(memory_space=pl.ANY)],
+        in_specs=[pl.BlockSpec(memory_space=pltpu.HBM)] * len(operands),
         out_specs=(vmem, vmem),
-        scratch_shapes=[
+        scratch_shapes=[pltpu.VMEM(operand.shape, F32) for operand in operands]
+        + [
+            pltpu.VMEM((rows, width), F32),
+            pltpu.VMEM((half, wide), F32),
             pltpu.VMEM((n_row, rows, width), F32),
-            pltpu.VMEM((n_col, w2.shape[0], wide), F32),
+            pltpu.VMEM((n_col, half, wide), F32),
             pltpu.VMEM((2, rows, seqs * factor), F32),
             pltpu.VMEM((n_col, rows, seqs * factor), F32),
             pltpu.VMEM((per, n_col, rows, seqs * factor), F32),
-            pltpu.VMEM(outer_weight.shape, F32),
             pltpu.VMEM((3 * factor, factor * z), BF16),
             pltpu.VMEM((all_seqs * factor, all_seqs * factor), BF16),
             pltpu.VMEM((rows * all_seqs, 128), F32),
@@ -358,14 +376,11 @@
             dma((n_col,)),
             dma((n_row,)),
             dma((per, n_col)),
-            dma(()),
+            dma((len(operands),)),
         ],
-        compiler_params=pltpu.CompilerParams(collective_id=0, has_side_effects=True),
-    )(
-        x2, w2, align_gain.reshape(1, -1), value_weight, gate_weight, output_weight,
-        outer_gain.reshape(1, -1), left_weight, right_weight, outer_weight,
-    )
-    pair_out = pair_state + update + outer_bias
+        compiler_params=pltpu.CompilerParams(collective_id=0, has_side_effects=True, vmem_limit_bytes=67043328 - 4 * rows * columns * z - (64 << 10)),
+    )(*operands)
+    pair_out = pair_state + update
     return (a_out.reshape(alignment.shape), pair_out)
 
 

time: 33.4 us -> 27 us (0.81)
  local copies, waits for them, and re-layouts: 5.17 us -> 0.71 us
  Pallas kernels: 24.6 us -> 23.5 us
  other arithmetic: 2.65 us -> 1.95 us
    unnamed x17 -> x2, local copies, waits for them, and re-layouts: 2.93 us -> 0.01 us
    pallas_call x1, Pallas kernels: 24.6 us -> 23.5 us  [on_device(): pl.pallas_call(functools.partial(kernel, n_row, n_col, heads, fold, colum...]
    slice x1 -> x0, local copies, waits for them, and re-layouts: 0.83 us -> none  [on_device(): w2 = jnp.concatenate([w2[a] for a in range(fold)], axis=1)]
    concatenate x1 -> x0, other arithmetic: 0.71 us -> none  [on_device(): w2 = jnp.concatenate([w2[a] for a in range(fold)], axis=1)]
    reshape x1 -> x0, local copies, waits for them, and re-layouts: 0.7 us -> none  [on_device(): x2 = alignment.reshape(rows, width)]
where the time goes in v2:
time: 27 us; the launch traced here: 26.8 us
  Pallas kernels  23.5 us (87%)
  other arithmetic  1.95 us (7%)
  local copies, waits for them, and re-layouts  0.71 us (3%)
  between operations  0.65 us (2%)
    pallas_call x1, Pallas kernels, on_device(): pl.pallas_call(functools.partial(kernel, n_row, n_col, heads, fold, colum...  23.5 us
    add x1, other arithmetic, on_device(): pair_out = pair_state + update  1.95 us
    reshape x1, local copies, waits for them, and re-layouts, on_device(): return (a_out.reshape(alignment.shape), pair_out)  0.7 us

profile of v2, /device:TPU:0, one launch (start us, length us, event | category | flops | bytes accessed | tf_op | source)
XLA Modules:
  0.0 26.8 jit_solution(1007043902896300294)
XLA Ops:
  0.6 23.5 %msa_block.1 = (f32[24,256]{1,0:T(8,128)}, f32[24,48,128]{2,1,0:T(8,128)S(1)}) custom-call(f32[24,4,64]{2,1,0:T(4,128)} %refs_0_.1, f32[192,48]{1,0:T(8,128)} %bitcast.7, f32[1,64]{1,0:T(1,128)} %bitcast.11, f32[64,256]{1,0:T(8,128)} %refs_3_.1, f32[64,256]{1,0:T(8,128)} %refs_4_.1, f32[64,256]{1,0:T(8,128)} %bitcast.8, f32[1,64]{1,0:T(1,128)} %bitcast.12, ...), custom_call_target="tpu_custom_call" | custom-call | tf_op jit(solution)/shard_map/msa_block/pallas_call | solution.py:344
  24.1 0.0 copy-start
  24.1 1.9 %add.3 = f32[24,48,128]{2,1,0:T(8,128)} add(f32[24,48,128]{2,1,0:T(8,128)} %param.13, f32[24,48,128]{2,1,0:T(8,128)S(1)} %get-tuple-element.5) | non-fusion elementwise | flops 147456 | bytes 1769472 | tf_op jit(solution)/shard_map/add | solution.py:383
  26.1 0.0 copy-done
  26.1 0.7 %reshape.23 = f32[24,4,64]{2,1,0:T(4,128)} reshape(f32[24,256]{1,0:T(8,128)S(1)} %copy-done) | data formatting | bytes 49152 | tf_op jit(solution)/shard_map/reshape | solution.py:384
Async XLA Ops:
  24.1 2.0 %copy-start = (f32[24,256]{1,0:T(8,128)S(1)}, f32[24,256]{1,0:T(8,128)}, u32[]{:S(2)}) copy-start(f32[24,256]{1,0:T(8,128)} %get-tuple-element.4) | copy-start | bytes 73732

commit v3 on v2

--- a/solution.py
+++ b/solution.py
@@ -58,13 +58,13 @@
 
 
 def kernel(n_row, n_col, heads, fold, columns, *refs):
-    inputs, (a_out, upd_out), local = refs[:11], refs[11:13], refs[13:24]
-    x_in, w_in, ag_ref, v_ref, g_ref, ot_ref, og_ref, lwt_ref, rwt_ref, bias_ref, ow = local
+    inputs, (a_out, upd_out), local = refs[:12], refs[12:14], refs[14:26]
+    x_in, w_in, ag_ref, v_ref, g_ref, ot_ref, og_ref, lwt_ref, rwt_ref, bias_ref, ow, pair = local
     (
     x_ref, w_ref, xbuf, wbuf, lr, lbuf, rbuf, wp, perm, lp, th, tl,
     bd_v, bd_g, bd_o, bd_lr,
     sx, rx, sw, rws, sl, rl, sr, rr, in_sem,
-    ) = refs[24:]
+    ) = refs[26:]
     r, c = lax.axis_index("row"), lax.axis_index("col")
     rows, width = x_ref.shape
     channels = v_ref.shape[0]
@@ -131,7 +131,7 @@
 
     xbuf[r] = x_ref[...]
     wbuf[c] = w_ref[...]
-    for load in loads[2:]:
+    for load in loads[2:-1]:
         load.wait()
     part = v_ref.shape[1] // fold
     o_w = ot_ref[...].T
@@ -213,7 +213,8 @@
         for hh in range(hpart):
             avg = jnp.where(head_of == hh, full[hh * rows : (hh + 1) * rows], avg)
         res = res + dot3(gates[a] * avg, bd_o[a, 0], bd_o[a, 1])
-    a_out[...] = res
+    for s in range(seqs):
+        a_out[:, s, :] = res[:, s * channels : (s + 1) * channels]
     both = dot3(normalize(res, out_gain), bd_lr[0], bd_lr[1])
     lr[0] = both[:, :lanes]
     lr[1] = both[:, lanes:]
@@ -289,9 +290,10 @@
     def finish(first):
         for q in range(pairs):
             u = fold_rows(dot(right2, th[q])) + dot(right1, tl[q]) + bias2
-            upd_out[first + 2 * q] = u[:, :z]
-            upd_out[first + 2 * q + 1] = u[:, z:]
-
+            upd_out[first + 2 * q] = pair[first + 2 * q] + u[:, :z]
+            upd_out[first + 2 * q + 1] = pair[first + 2 * q + 1] + u[:, z:]
+
+    loads[-1].wait()
     finish(0)
     if rows > block:
 
@@ -340,12 +342,13 @@
         alignment, pair_weights.reshape(heads * rows, columns), align_gain.reshape(1, -1),
         value_weight, gate_weight, output_weight.T, outer_gain.reshape(1, -1),
         left_weight.T, right_weight.T, outer_bias.reshape(1, -1), outer_weight,
+        pair_state,
     )
-    a_out, update = pl.pallas_call(
+    return pl.pallas_call(
         functools.partial(kernel, n_row, n_col, heads, fold, columns),
         name="msa_block",
         out_shape=(
-            jax.ShapeDtypeStruct((rows, width), F32),
+            pltpu.VMEM(alignment.shape, F32),
             pltpu.VMEM((rows, columns, z), F32),
         ),
         in_specs=[pl.BlockSpec(memory_space=pltpu.HBM)] * len(operands),
@@ -380,8 +383,6 @@
         ],
         compiler_params=pltpu.CompilerParams(collective_id=0, has_side_effects=True, vmem_limit_bytes=67043328 - 4 * rows * columns * z - (64 << 10)),
     )(*operands)
-    pair_out = pair_state + update
-    return (a_out.reshape(alignment.shape), pair_out)
 
 
 def solution(mesh):

time: 27 us -> 25.2 us (0.933)
  other arithmetic: 1.95 us -> 0 us
  local copies, waits for them, and re-layouts: 0.71 us -> 1.44 us
  Pallas kernels: 23.5 us -> 23 us
    add x1 -> x0, other arithmetic: 1.95 us -> none  [on_device(): pair_out = pair_state + update]
    unnamed x2, local copies, waits for them, and re-layouts: 0.01 us -> 1.44 us
    reshape x1 -> x0, local copies, waits for them, and re-layouts: 0.7 us -> none  [on_device(): return (a_out.reshape(alignment.shape), pair_out)]
    pallas_call x1, Pallas kernels: 23.5 us -> 23 us  [on_device(): pl.pallas_call(functools.partial(kernel, n_row, n_col, heads, fold, colum...]
where the time goes in v3:
time: 25.2 us; the launch traced here: 25 us
  Pallas kernels  23 us (91%)
  local copies, waits for them, and re-layouts  1.44 us (6%)
  between operations  0.64 us (3%)
    pallas_call x1, Pallas kernels, on_device(): pl.pallas_call(functools.partial(kernel, n_row, n_col, heads, fold, colum...  23 us
    unnamed x2, local copies, waits for them, and re-layouts  1.44 us

profile of v3, /device:TPU:0, one launch (start us, length us, event | category | flops | bytes accessed | tf_op | source)
XLA Modules:
  0.0 25.0 jit_solution(10902068949851217822)
XLA Ops:
  0.6 23.0 %msa_block.1 = (f32[24,4,64]{2,1,0:T(4,128)S(1)}, f32[24,48,128]{2,1,0:T(8,128)S(1)}) custom-call(f32[24,4,64]{2,1,0:T(4,128)} %refs_0_.1, f32[192,48]{1,0:T(8,128)} %bitcast.7, f32[1,64]{1,0:T(1,128)} %bitcast.11, f32[64,256]{1,0:T(8,128)} %refs_3_.1, f32[64,256]{1,0:T(8,128)} %refs_4_.1, f32[64,256]{1,0:T(8,128)} %bitcast.8, f32[1,64]{1,0:T(1,128)} %bitcast.12, ...), custom_call_target="tpu_custom_call" | custom-call | tf_op jit(solution)/shard_map/msa_block/pallas_call | solution.py:347
  23.6 0.6 %copy.16 = f32[24,4,64]{2,1,0:T(4,128)} copy(f32[24,4,64]{2,1,0:T(4,128)S(1)} %get-tuple-element.2) | data formatting | bytes 49152
  24.2 0.8 %copy.17 = f32[24,48,128]{2,1,0:T(8,128)} copy(f32[24,48,128]{2,1,0:T(8,128)S(1)} %get-tuple-element.3) | data formatting | bytes 1179648
